TPU v7x, 256 devices: a whole 4x4x8 slice. The times are simulated.
256 devices in a mesh: grp: 32 (over y, x, core), mem: 8 (over z).
Axes of the slice: x: 4, y: 4, z: 8, core: 2. Of those that a mesh axis runs over, the one named last changes fastest.
Arguments:
- features: bfloat16 [131072, 512], P(('grp', 'mem')), may hold values from -6 to 6
- weight: bfloat16 [512, 512], replicated, may hold values from -0.25 to 0.25
- adj_tiles: bfloat16 [1024, 32, 128, 128], P(('grp', 'mem')), may hold values from -0.09375 to 0.09375
- adj_cols: int32 [1024, 32], P(('grp', 'mem')), may hold values from 0 to 31
- send_blocks: int32 [256, 32, 2], P(('grp', 'mem')), may hold values from -1 to 3, as said below
- read_tiles: bfloat16 [256, 32, 2, 128, 128], P(('grp', 'mem')), may hold values from -0.1875 to 0.1875
- read_rows: int32 [256, 32, 2], P(('grp', 'mem')), may hold values from 0 to 3
Outputs:
- output: bfloat16 [131072, 512], P(('grp', 'mem'))
Inputs may be any that keep to these rules, and one draw needn't show every extreme that they name: `send_blocks`: -1 marks an empty slot; the used slots of each entry come first. In every draw, for each m some group receives 2 blocks from every vertex block s * 8 + m.
All inputs are finite; a program needn't handle non-finite values.
Results may differ from a plain program's by a relative error of at most 0.0058.
Values may be sent and summed in bfloat16 or wider, within the bound.
No kernel may reach another device: no remote copies, remote signals or barrier semaphores. Data moves between devices by JAX's collectives and lax.ppermute only.
A program may use at most 128 MiB of HBM per device.

v0:
```python
import jax
import jax.numpy as jnp
from jax import lax
from jax.sharding import PartitionSpec as P


def per_device(features, weight, adj_tiles, adj_cols, send_blocks, read_tiles, read_rows):
    rows_here = features.shape[0]
    width = features.shape[1]
    tile_rows = adj_tiles.shape[2]
    block_count = rows_here // tile_rows
    group_rows = lax.all_gather(features, "mem", axis=0, tiled=True)
    group_tiles = group_rows.reshape(-1, tile_rows, width)
    chosen = jnp.take(group_tiles, adj_cols, axis=0)
    propagated = jnp.einsum("rkij,rkjf->rif", adj_tiles, chosen, preferred_element_type=jnp.float32)
    propagated = propagated.astype(jnp.bfloat16).reshape(rows_here, width)
    hidden = jnp.maximum(
        jnp.dot(propagated, weight, preferred_element_type=jnp.float32), 0.0
    ).astype(jnp.bfloat16)
    slot_lists = send_blocks[0]
    tiles_in = read_tiles[0]
    onehot = (
        read_rows[0][:, :, None] == jnp.arange(block_count, dtype=jnp.int32)[None, None, :]
    ).astype(jnp.float32)
    wanted = lax.all_to_all(slot_lists, "grp", split_axis=0, concat_axis=0, tiled=True)
    shard_rows = lax.all_gather(hidden, "grp", axis=0, tiled=True)
    group_count = shard_rows.shape[0] // rows_here
    pieces = shard_rows.reshape(group_count, block_count, tile_rows, width)
    safe_lists = jnp.clip(wanted, 0, block_count - 1)
    picked = pieces[jnp.arange(group_count, dtype=jnp.int32)[:, None], safe_lists]
    picked = jnp.where((wanted >= 0)[:, :, None, None], picked, jnp.zeros((), jnp.bfloat16))
    products = jnp.einsum("gkij,gkjf->gkif", tiles_in, picked, preferred_element_type=jnp.float32)
    aggregate = jnp.einsum("gkr,gkif->rif", onehot, products, precision=lax.Precision.HIGHEST)
    combined = hidden.astype(jnp.float32) + aggregate.reshape(rows_here, width)
    return combined.astype(jnp.bfloat16)


def solution(mesh):
    placed = (
        P(("grp", "mem"), None),
        P(),
        P(("grp", "mem"), None, None, None),
        P(("grp", "mem"), None),
        P(("grp", "mem"), None, None),
        P(("grp", "mem"), None, None, None, None),
        P(("grp", "mem"), None, None),
    )
    return jax.shard_map(
        per_device, mesh=mesh, in_specs=placed, out_specs=P(("grp", "mem"), None), check_vma=False
    )
```

profile of v0, /device:TPU:1, one launch (start us, length us, event | category | flops | bytes accessed | tf_op | source)
XLA Modules:
  0.0 239.2 jit_solution(8391985096716967767)
XLA Ops:
  6.5 0.0 copy-start
  6.5 0.0 all-gather.3.cloned.1.call-start
  6.5 0.7 all-gather.3.cloned.1.call-update
  7.3 0.0 all-gather.5.cloned.1.call-start
  7.3 0.7 compare_select_fusion
  8.0 0.1 reshape.58
  8.1 0.7 compare_and_fusion
  8.8 58.8 %all-gather.3.cloned.1.call-done = bf16[4096,512]{1,0:T(8,128)(2,1)} async-done(((bf16[512,512]{1,0:T(8,128)(2,1)}), bf16[4096,512]{1,0:T(8,128)(2,1)}) %all-gather.3.cloned.1.call-update) | async-done | bytes 4194320 | tf_op jit(solution)/shard_map/all_gather | solution.py:12
  67.5 10.5 %gather_fusion = bf16[128,128,512]{2,1,0:T(8,128)(2,1)} fusion(bf16[32,128,512]{2,1,0:T(8,128)(2,1)} %bitcast.39, s32[1024]{0:T(1024)S(1)} %pad_clamp_fusion), kind=kCustom, calls=%fused_computation | custom fusion | bytes 33554944 | tf_op jit(solution)/shard_map/jit(_take)/gather | solution.py:14
  78.0 0.0 copy-start.4
  78.0 0.0 copy-start.3
  78.0 10.4 %fusion.11 = bf16[4,512,128]{1,2,0:T(8,128)(2,1)S(1)} fusion(bf16[4,32,128,128]{3,2,1,0:T(8,128)(2,1)} %param.9, bf16[4,32,128,512]{3,2,1,0:T(8,128)(2,1)} %bitcast.41, pred[4,32]{1,0:T(4,128)(4,1)S(1)} %compare_and_fusion), kind=kOutput, calls=%fused_computation.14 | convolution fusion | flops 2156134400 | bytes 21495936 | tf_op jit(solution)/shard_map/rkij,rkjf->rif/dot_general | solution.py:15
  88.4 0.0 copy-done.4
  88.4 1.2 fusion.14
  89.7 0.0 all-gather.5.cloned.1.call-update
  89.7 0.0 copy-done.3
  89.7 0.1 copy.22
  89.8 14.5 %all_to_all.9 = s32[32,1,2]{2,1,0:T(1,128)S(1)} all-to-all(s32[32,1,2]{2,1,0:T(1,128)S(1)} %copy.22), channel_id=1, replica_groups=mesh['grp'=32,'mem'=8] {'grp'}, dimensions={0} | all-to-all | bytes 512 | tf_op jit(solution)/shard_map/all_to_all | solution.py:25
  104.3 0.1 copy.23
  104.4 0.1 copy.24
  104.5 0.1 copy.26
  104.6 0.1 reshape.64
  104.7 61.9 %all-gather.5.cloned.1.call-done = bf16[16384,512]{1,0:T(8,128)(2,1)} async-done(((bf16[512,512]{1,0:T(8,128)(2,1)}), bf16[16384,512]{1,0:T(8,128)(2,1)}) %all-gather.5.cloned.1.call-update) | async-done | bytes 16777232 | tf_op jit(solution)/shard_map/all_gather | solution.py:26
  166.6 11.6 %gather_fusion.1 = bf16[64,128,512]{2,1,0:T(8,128)(2,1)} fusion(bf16[32,4,128,512]{3,2,1,0:T(8,128)(2,1)} %bitcast.42, s32[64]{0:T(128)S(1)} %reshape.64), kind=kCustom, calls=%fused_computation.1 | custom fusion | bytes 16777728 | tf_op jit(solution)/shard_map/gather | solution.py:30
  178.2 11.9 %copy.27 = bf16[64,128,512]{1,2,0:T(8,128)(2,1)} copy(bf16[64,128,512]{2,1,0:T(8,128)(2,1)} %gather_fusion.1) | data formatting | bytes 16777216 | tf_op jit(solution)/shard_map/gather | solution.py:30
  190.1 0.0 copy-done
  190.1 11.5 %convolution_bitcast_fusion = f32[32,2,128,512]{2,3,1,0:T(8,128)} fusion(bf16[32,2,128,512]{2,3,1,0:T(8,128)(2,1)} %bitcast.40, pred[32,2]{1,0:T(8,128)(4,1)S(1)} %copy.24, bf16[1,32,2,128,128]{4,3,2,1,0:T(8,128)(2,1)S(1)} %copy-done), kind=kOutput, calls=%fused_computation.5 | convolution fusion | flops 1077936128 | bytes 27263040 | tf_op jit(solution)/shard_map/gkij,gkjf->gkif/dot_general | solution.py:32
  201.6 0.0 copy-start.2
  201.6 20.0 %copy.28 = f32[32,2,128,512]{3,0,1,2:T(8,128)} copy(f32[32,2,128,512]{2,3,1,0:T(8,128)} %convolution_bitcast_fusion) | data formatting | bytes 33554432 | tf_op jit(solution)/shard_map/gkij,gkjf->gkif/dot_general | solution.py:32
  221.6 0.0 copy-done.2
  221.6 0.0 copy-start.1
  221.6 9.4 %convolution_bitcast_fusion.1 = f32[4,128,512]{2,0,1:T(4,128)S(1)} fusion(f32[32,2,128,512]{3,0,1,2:T(8,128)} %copy.28, s32[32,2]{0,1:T(2,128)S(1)} %bitcast.43), kind=kOutput, calls=%fused_computation.11 | convolution fusion | flops 201326848 | bytes 17826048 | tf_op jit(solution)/shard_map/gkr,gkif->rif/dot_general | solution.py:33
  231.0 0.3 copy.29
  231.4 0.0 copy-done.1
  231.4 1.0 fusion.15
  (3 shorter events, 0.0 us)
Async XLA Ops:
  6.5 183.6 %copy-start = (bf16[1,32,2,128,128]{4,3,2,1,0:T(8,128)(2,1)S(1)}, bf16[1,32,2,128,128]{4,3,2,1,0:T(8,128)(2,1)}, u32[]{:S(2)}) copy-start(bf16[1,32,2,128,128]{4,3,2,1,0:T(8,128)(2,1)} %param.12) | copy-start | bytes 6291460
  6.5 61.0 %all-gather.3.cloned.1.call-start = ((), (), s32[]{:S(2)}) async-start(), calls=%async_computation.1 | async-start | bytes 4718592 | tf_op jit(solution)/shard_map/all_gather | solution.py:12
  7.3 159.3 %all-gather.5.cloned.1.call-start = ((), (), s32[]{:S(2)}) async-start(), calls=%async_computation.2 | async-start | bytes 17301504 | tf_op jit(solution)/shard_map/all_gather | solution.py:26
  78.0 10.4 %copy-start.4 = (bf16[512,512]{1,0:T(8,128)(2,1)S(1)}, bf16[512,512]{1,0:T(8,128)(2,1)}, u32[]{:S(2)}) copy-start(bf16[512,512]{1,0:T(8,128)(2,1)} %param.8) | copy-start | bytes 1572868
  78.0 11.7 %copy-start.3 = (s32[1,32,2]{1,2,0:T(2,128)S(1)}, s32[1,32,2]{1,2,0:T(2,128)}, u32[]{:S(2)}) copy-start(s32[1,32,2]{1,2,0:T(2,128)} %param.11) | copy-start | bytes 772
  201.6 20.0 %copy-start.2 = (s32[1,32,2]{1,2,0:T(2,128)S(1)}, s32[1,32,2]{1,2,0:T(2,128)}, u32[]{:S(2)}) copy-start(s32[1,32,2]{1,2,0:T(2,128)} %param.13) | copy-start | bytes 772
  221.6 9.8 %copy-start.1 = (bf16[512,512]{1,0:T(8,128)(2,1)S(1)}, bf16[512,512]{1,0:T(8,128)(2,1)}, u32[]{:S(2)}) copy-start(bf16[512,512]{1,0:T(8,128)(2,1)} %fusion.14) | copy-start | bytes 1572868
Sparse Core Ops, SparseCore 0:
  9.1 58.3 all-gather.2
  89.8 76.7 all-gather.4
where the time goes:
time: 240 us; the launch traced here: 239 us
  waiting for transfers between devices  121 us (50%)
  local copies, waits for them, and re-layouts  54.9 us (23%)
  matrix products  32.5 us (14%)
  blocking collectives  14.5 us (6%)
  between operations  13.5 us (6%)
    all_gather x1, waiting for transfers between devices, per_device(): shard_rows = lax.all_gather(hidden, 'grp', axis=0, tiled=True)  61.9 us
    all_gather x1, waiting for transfers between devices, per_device(): group_rows = lax.all_gather(features, 'mem', axis=0, tiled=True)  58.8 us
    gather x2, local copies, waits for them, and re-layouts, per_device(): pieces[jnp.arange(group_count, dtype=jnp.int32)[:, None], safe_lists]  23.5 us
    dot_general x1, local copies, waits for them, and re-layouts, per_device(): jnp.einsum('gkij,gkjf->gkif', tiles_in, picked, preferred_element_type=jn...  20 us
    all_to_all x1, blocking collectives, per_device(): lax.all_to_all(slot_lists, 'grp', split_axis=0, concat_axis=0, tiled=True)  14.5 us
    dot_general x1, matrix products, per_device(): jnp.einsum('gkij,gkjf->gkif', tiles_in, picked, preferred_element_type=jn...  11.5 us
    gather x1, local copies, waits for them, and re-layouts, per_device(): chosen = jnp.take(group_tiles, adj_cols, axis=0)  10.5 us
    dot_general x1, matrix products, per_device(): jnp.einsum('rkij,rkjf->rif', adj_tiles, chosen, preferred_element_type=jn...  10.4 us
  transfers between devices with their start and end apart: 2, of which 2 were waited for; matrix products, arithmetic and copies ran while one was open for 1% of the time, Pallas kernels for 0%

commit v1 on v0

--- a/solution.py
+++ b/solution.py
@@ -23,7 +23,9 @@
         read_rows[0][:, :, None] == jnp.arange(block_count, dtype=jnp.int32)[None, None, :]
     ).astype(jnp.float32)
     wanted = lax.all_to_all(slot_lists, "grp", split_axis=0, concat_axis=0, tiled=True)
-    shard_rows = lax.all_gather(hidden, "grp", axis=0, tiled=True)
+    shard_rows = jnp.concatenate(
+        lax.all_to_all(jnp.stack([hidden] * lax.axis_size("grp")), "grp", 0, 0), axis=0
+    )
     group_count = shard_rows.shape[0] // rows_here
     pieces = shard_rows.reshape(group_count, block_count, tile_rows, width)
     safe_lists = jnp.clip(wanted, 0, block_count - 1)

time: 240 us -> 387 us (1.61)
  the two profiles are of different devices: /device:TPU:1 before, /device:TPU:96 now
where the time goes in v1:
time: 387 us; the launch traced here: 386 us
  waiting for transfers between devices  261 us (67%)
  local copies, waits for them, and re-layouts  62.1 us (16%)
  matrix products  31.7 us (8%)
  starting transfers between devices  14.7 us (4%)
  between operations  13.5 us (3%)
    all_to_all x1, waiting for transfers between devices, per_device(): lax.all_to_all(jnp.stack([hidden] * lax.axis_size('grp')), 'grp', 0, 0)  213 us
    all_gather x1, waiting for transfers between devices, per_device(): group_rows = lax.all_gather(features, 'mem', axis=0, tiled=True)  47.8 us
    gather x2, local copies, waits for them, and re-layouts, per_device(): pieces[jnp.arange(group_count, dtype=jnp.int32)[:, None], safe_lists]  23.5 us
    dot_general x1, local copies, waits for them, and re-layouts, per_device(): jnp.einsum('gkij,gkjf->gkif', tiles_in, picked, preferred_element_type=jn...  20 us
    dot_general x1, matrix products, per_device(): jnp.einsum('gkij,gkjf->gkif', tiles_in, picked, preferred_element_type=jn...  11.5 us
    gather x1, local copies, waits for them, and re-layouts, per_device(): chosen = jnp.take(group_tiles, adj_cols, axis=0)  10.5 us
    dot_general x1, matrix products, per_device(): jnp.einsum('rkij,rkjf->rif', adj_tiles, chosen, preferred_element_type=jn...  10.4 us
    dot_general x1, matrix products, per_device(): jnp.einsum('gkr,gkif->rif', onehot, products, precision=lax.Precision.HIG...  9.34 us
  transfers between devices with their start and end apart: 3, of which 2 were waited for; matrix products, arithmetic and copies ran while one was open for 6% of the time, Pallas kernels for 0%

profile of v1, /device:TPU:96, one launch (start us, length us, event | category | flops | bytes accessed | tf_op | source)
XLA Modules:
  0.0 385.5 jit_solution(12342572484486253613)
XLA Ops:
  6.5 0.0 copy-start
  6.5 0.0 all-gather.2.cloned.1.call-start
  6.5 0.7 all-gather.2.cloned.1.call-update
  7.3 1.4 copy.29
  8.6 7.3 %all-to-all-start = ((s32[32,1,2]{2,1,0:T(1,128)}), s32[32,1,2]{2,1,0:T(1,128)S(1)}, u32[]{:S(2)}, u32[]{:S(2)}) async-start(s32[32,1,2]{2,1,0:T(1,128)} %copy.29), calls=%async_computation | async-start | bytes 32768 | tf_op jit(solution)/shard_map/all_to_all | solution.py:25
  15.9 0.7 compare_select_fusion
  16.6 0.1 reshape.56
  16.7 0.7 compare_and_fusion
  17.4 47.8 %all-gather.2.cloned.1.call-done = bf16[4096,512]{1,0:T(8,128)(2,1)} async-done(((bf16[512,512]{1,0:T(8,128)(2,1)}), bf16[4096,512]{1,0:T(8,128)(2,1)}) %all-gather.2.cloned.1.call-update) | async-done | bytes 4194320 | tf_op jit(solution)/shard_map/all_gather | solution.py:12
  65.2 10.5 %gather_fusion = bf16[128,128,512]{2,1,0:T(8,128)(2,1)} fusion(bf16[32,128,512]{2,1,0:T(8,128)(2,1)} %bitcast.39, s32[1024]{0:T(1024)S(1)} %pad_clamp_fusion), kind=kCustom, calls=%fused_computation | custom fusion | bytes 33554944 | tf_op jit(solution)/shard_map/jit(_take)/gather | solution.py:14
  75.7 0.0 copy-start.2
  75.7 10.4 %fusion.11 = bf16[4,512,128]{1,2,0:T(8,128)(2,1)S(1)} fusion(bf16[4,32,128,128]{3,2,1,0:T(8,128)(2,1)} %param.9, bf16[4,32,128,512]{3,2,1,0:T(8,128)(2,1)} %bitcast.41, pred[4,32]{1,0:T(4,128)(4,1)S(1)} %compare_and_fusion), kind=kOutput, calls=%fused_computation.14 | convolution fusion | flops 2156134400 | bytes 21495936 | tf_op jit(solution)/shard_map/rkij,rkjf->rif/dot_general | solution.py:15
  86.1 0.0 copy-done.2
  86.1 0.4 fusion.14
  86.5 0.0 all-to-all-done
  86.6 5.9 %stack.2 = bf16[32,512,512]{2,1,0:T(8,128)(2,1)} broadcast(bf16[512,512]{1,0:T(8,128)(2,1)S(1)} %fusion.14), dimensions={1,2} | broadcast | bytes 17301504 | tf_op jit(solution)/shard_map/stack | solution.py:27
  92.5 7.4 %all-to-all-start.1 = ((bf16[32,512,512]{2,1,0:T(8,128)(2,1)}), bf16[32,512,512]{2,1,0:T(8,128)(2,1)}, u32[]{:S(2)}, u32[]{:S(2)}) async-start(bf16[32,512,512]{2,1,0:T(8,128)(2,1)} %stack.2), calls=%async_computation.1 | async-start | bytes 33554432 | tf_op jit(solution)/shard_map/all_to_all | solution.py:27
  99.9 0.1 copy.30
  100.0 0.1 copy.33
  100.1 0.1 reshape.62
  100.2 0.1 copy.31
  100.3 212.7 %all-to-all-done.1 = bf16[32,512,512]{2,1,0:T(8,128)(2,1)} async-done(((bf16[32,512,512]{2,1,0:T(8,128)(2,1)}), bf16[32,512,512]{2,1,0:T(8,128)(2,1)}, u32[]{:S(2)}, u32[]{:S(2)}) %all-to-all-start.1) | async-done | bytes 16777248 | tf_op jit(solution)/shard_map/all_to_all | solution.py:27
  313.0 11.6 %gather_fusion.1 = bf16[64,128,512]{2,1,0:T(8,128)(2,1)} fusion(bf16[32,4,128,512]{3,2,1,0:T(8,128)(2,1)} %bitcast.10, s32[64]{0:T(128)S(1)} %reshape.62), kind=kCustom, calls=%fused_computation.1 | custom fusion | bytes 16777728 | tf_op jit(solution)/shard_map/gather | solution.py:32
  324.6 11.9 %copy.34 = bf16[32,2,128,512]{2,3,1,0:T(8,128)(2,1)} copy(bf16[32,2,128,512]{3,2,1,0:T(8,128)(2,1)} %bitcast.40) | data formatting | bytes 16777216 | tf_op jit(solution)/shard_map/gather | solution.py:32
  336.5 0.0 copy-done
  336.5 11.5 %convolution_bitcast_fusion = f32[32,2,128,512]{2,3,1,0:T(8,128)} fusion(bf16[32,2,128,512]{2,3,1,0:T(8,128)(2,1)} %copy.34, pred[32,2]{1,0:T(8,128)(4,1)S(1)} %copy.31, bf16[1,32,2,128,128]{4,3,2,1,0:T(8,128)(2,1)S(1)} %copy-done), kind=kOutput, calls=%fused_computation.5 | convolution fusion | flops 1077936128 | bytes 27263040 | tf_op jit(solution)/shard_map/gkij,gkjf->gkif/dot_general | solution.py:34
  348.0 0.0 copy-start.1
  348.0 20.0 %copy.35 = f32[32,2,128,512]{3,0,1,2:T(8,128)} copy(f32[32,2,128,512]{2,3,1,0:T(8,128)} %convolution_bitcast_fusion) | data formatting | bytes 33554432 | tf_op jit(solution)/shard_map/gkij,gkjf->gkif/dot_general | solution.py:34
  368.0 0.0 copy-done.1
  368.0 9.3 %convolution_bitcast_fusion.1 = f32[4,128,512]{2,0,1:T(4,128)S(1)} fusion(f32[32,2,128,512]{3,0,1,2:T(8,128)} %copy.35, s32[32,2]{0,1:T(2,128)S(1)} %bitcast.42), kind=kOutput, calls=%fused_computation.11 | convolution fusion | flops 201326848 | bytes 17826048 | tf_op jit(solution)/shard_map/gkr,gkif->rif/dot_general | solution.py:35
  377.3 0.3 copy.36
  377.7 1.0 fusion.15
  (3 shorter events, 0.0 us)
Async XLA Ops:
  6.5 329.9 %copy-start = (bf16[1,32,2,128,128]{4,3,2,1,0:T(8,128)(2,1)S(1)}, bf16[1,32,2,128,128]{4,3,2,1,0:T(8,128)(2,1)}, u32[]{:S(2)}) copy-start(bf16[1,32,2,128,128]{4,3,2,1,0:T(8,128)(2,1)} %param.12) | copy-start | bytes 6291460
  6.5 58.7 %all-gather.2.cloned.1.call-start = ((), (), s32[]{:S(2)}) async-start(), calls=%async_computation.2 | async-start | bytes 4718592 | tf_op jit(solution)/shard_map/all_gather | solution.py:12
  8.6 77.9 %all-to-all-start = ((s32[32,1,2]{2,1,0:T(1,128)}), s32[32,1,2]{2,1,0:T(1,128)S(1)}, u32[]{:S(2)}, u32[]{:S(2)}) async-start(s32[32,1,2]{2,1,0:T(1,128)} %copy.29), calls=%async_computation | async-start | bytes 32768 | tf_op jit(solution)/shard_map/all_to_all | solution.py:25
  75.7 10.4 %copy-start.2 = (bf16[512,512]{1,0:T(8,128)(2,1)S(1)}, bf16[512,512]{1,0:T(8,128)(2,1)}, u32[]{:S(2)}) copy-start(bf16[512,512]{1,0:T(8,128)(2,1)} %param.8) | copy-start | bytes 1572868
  92.5 220.5 %all-to-all-start.1 = ((bf16[32,512,512]{2,1,0:T(8,128)(2,1)}), bf16[32,512,512]{2,1,0:T(8,128)(2,1)}, u32[]{:S(2)}, u32[]{:S(2)}) async-start(bf16[32,512,512]{2,1,0:T(8,128)(2,1)} %stack.2), calls=%async_computation.1 | async-start | bytes 33554432 | tf_op jit(solution)/shard_map/all_to_all | solution.py:27
  348.0 20.0 %copy-start.1 = (s32[1,32,2]{1,2,0:T(2,128)S(1)}, s32[1,32,2]{1,2,0:T(2,128)}, u32[]{:S(2)}) copy-start(s32[1,32,2]{1,2,0:T(2,128)} %param.13) | copy-start | bytes 772
Sparse Core Ops, SparseCore 0:
  9.1 56.0 all-gather.1
